TPU v7x, 32 devices: a whole 2x2x4 slice. The times are simulated.
32 devices in a mesh: tm: 8 (over y, x, core), space: 4 (over z).
Axes of the slice: x: 2, y: 2, z: 4, core: 2. Of those that a mesh axis runs over, the one named last changes fastest.
Arguments:
- coarse_guess: float32 [8, 32, 12, 512], P('tm', 'space'), may hold values from -6 to 6
- initial_state: float32 [32, 12, 512], P('space'), may hold values from -6 to 6
- fine_volume: bfloat16 [512, 512], replicated
- coarse_volume: bfloat16 [512, 512], replicated
- lift_matrix: bfloat16 [384, 512], replicated, may hold values from -0.0390625 to 0.0390625
- wave_speed: float32 [12], replicated, may hold values from 0.1 to 0.6
- reaction_rate: float32 [24], replicated, may hold values from 0.05 to 0.5
- species_map: int32 [24, 3], replicated, may hold values from 0 to 11
- neighbour_element: int32 [32, 6], P('space'), may hold values from 0 to 7
- neighbour_rank: int32 [32, 6], P('space'), may hold values from -1 to 1
Outputs:
- iterate: float32 [32, 32, 12, 512], P('tm', 'space')
All inputs are finite; a program needn't handle non-finite values.
Results may differ from a plain program's by a relative error of at most 0.025.
Values may be sent and summed in bfloat16 or wider, within the bound.
A program may use at most 64 MiB of HBM per device.

v0:
```python
import functools

import jax
import jax.numpy as jnp
import numpy as np
from jax import lax
from jax.experimental import pallas as pl
from jax.experimental.pallas import tpu as pltpu
from jax.sharding import PartitionSpec as P

SIDE = 8
STRIDE = 4
COARSE_GAIN = 4.0
VMEM = pltpu.VMEM
SMEM = pltpu.SMEM
MESH = pl.DeviceIdType.MESH


def face_tables(side):
    plane = side * side
    inner = np.arange(plane)
    first, second = inner // side, inner % side
    last = side - 1
    node_lists = [
        first * side + second,
        last * plane + first * side + second,
        first * plane + second,
        first * plane + last * side + second,
        first * plane + second * side,
        first * plane + second * side + last,
    ]
    table = np.zeros((side**3, 12 * plane), np.float32)
    for f in range(6):
        table[node_lists[f], f * plane + inner] = 1.0
        table[node_lists[f ^ 1], (6 + f) * plane + inner] = 1.0
    return table


def find_jumps(speed, c, x_ref, g_ref, j_ref):
    variables = speed.shape[0]
    elems = x_ref.shape[0] // variables
    faces = c["table"].shape[1] // 2
    plane = faces // 6
    pair = 2 * plane
    both = jnp.dot(x_ref[...], c["table"][...], preferred_element_type=jnp.float32)
    lane = lax.broadcasted_iota(jnp.int32, (1, pair), 1)
    low = jnp.where(lane < plane, 1.0, 0.0)
    high = 1.0 - low
    for k in range(3):
        for v in range(variables):
            rows = slice(v * elems, (v + 1) * elems)
            swapped = both[rows, faces + k * pair : faces + (k + 1) * pair]
            cols = slice(v * pair, (v + 1) * pair)
            g_ref[k, 0:elems, cols] = (swapped * low).astype(jnp.bfloat16)
            g_ref[k, elems : 2 * elems, cols] = (swapped * high).astype(jnp.bfloat16)
    for k in range(3):
        across = jnp.dot(c["pick"][k], g_ref[k], preferred_element_type=jnp.float32)
        for v in range(variables):
            rows = slice(v * elems, (v + 1) * elems)
            own = both[rows, k * pair : (k + 1) * pair]
            jump = speed[v] * (across[:, v * pair : (v + 1) * pair] - own)
            j_ref[rows, k * pair : (k + 1) * pair] = jump.astype(jnp.bfloat16)


def transport_react(gain, volume, c, x_ref, j_ref, m_ref, a_ref):
    variables, elems, nodes = m_ref.shape
    moved = jnp.dot(x_ref[...], volume[...], preferred_element_type=jnp.float32)
    moved = moved + jnp.dot(j_ref[...], c["lift"][...], preferred_element_type=jnp.float32)
    moved = moved.reshape(m_ref.shape)
    m_ref[...] = moved
    a_ref[...] = moved
    species, rates = c["species"], c["rates"]
    for r in range(species.shape[0]):
        s0, s1, s2 = species[r, 0], species[r, 1], species[r, 2]
        a, b = m_ref[s0], m_ref[s1]
        rate = (rates[r] * gain) * (a * b) / (1.0 + a * a + b * b)
        a_ref[s2] += rate
        a_ref[s0] -= rate


def store_state(a_ref, x_ref):
    x_ref[...] = a_ref[...].reshape(x_ref.shape).astype(jnp.bfloat16)


CONSTS = ("table", "pick", "lift", "fine", "coarse", "speed", "rates", "species")
IN_SMEM = ("speed", "rates", "species")


def phase_scratch(variables, elems, nodes, faces):
    return [
        VMEM((variables * elems, nodes), jnp.bfloat16),
        VMEM((3, 2 * elems, variables * (faces // 3)), jnp.bfloat16),
        VMEM((variables * elems, faces), jnp.bfloat16),
        VMEM((variables, elems, nodes), jnp.float32),
        VMEM((variables, elems, nodes), jnp.float32),
    ]


def fine_substep(c, x, g, j, m, a):
    find_jumps(c["speed"], c, x, g, j)
    transport_react(1.0, c["fine"], c, x, j, m, a)
    store_state(a, x)


def loop(count, fn):
    def one(i, carry):
        fn(i)
        return carry

    lax.fori_loop(0, count, one, 0)


def phase_one(*refs):
    c = dict(zip(CONSTS, refs))
    start, out = refs[len(CONSTS) : len(CONSTS) + 2]
    x, g, j, m, a = refs[len(CONSTS) + 2 :]
    x[...] = start[...].reshape(x.shape)
    loop(2 * STRIDE, lambda i: fine_substep(c, x, g, j, m, a))
    out[...] = x[...].reshape(out.shape)


def phase_two(*refs):
    c = dict(zip(CONSTS, refs))
    row, second, corr, message = refs[len(CONSTS) : len(CONSTS) + 4]
    x, g, j, m, a = refs[len(CONSTS) + 4 :]
    x[...] = second[...].reshape(x.shape)
    find_jumps(c["speed"], c, x, g, j)
    transport_react(COARSE_GAIN, c["coarse"], c, x, j, m, a)
    corr[...] = a[...]
    loop(2 * STRIDE, lambda i: fine_substep(c, x, g, j, m, a))
    keep = jnp.where(row[0] == 1, 0.0, 1.0)
    message[...] = (a[...] - keep * corr[...]).astype(jnp.bfloat16)
    corr[...] = a[...] - corr[...]


def phase_three(*refs):
    c = dict(zip(CONSTS, refs))
    row, second, corr, messages, out = refs[len(CONSTS) : len(CONSTS) + 5]
    x, g, j, m, a = refs[len(CONSTS) + 5 :]
    here = row[0]
    block = out.shape[2]
    own = pl.ds(pl.multiple_of(row[1] * block, block), block)

    @pl.when(here < 2)
    def _():
        x[...] = second[...].reshape(x.shape)

    @pl.when(here >= 2)
    def _():
        x[...] = messages[1].reshape(x.shape)

    def coarse():
        find_jumps(c["speed"], c, x, g, j)
        transport_react(COARSE_GAIN, c["coarse"], c, x, j, m, a)

    def advance(i, carry):
        coarse()
        a[...] += messages[i].astype(jnp.float32)
        store_state(a, x)
        return carry

    lax.fori_loop(2, here, advance, 0)
    coarse()
    out[STRIDE - 1] = a[:, own, :] + corr[:, own, :]

    def point(k):
        loop(2, lambda i: fine_substep(c, x, g, j, m, a))
        out[k] = a[:, own, :]

    loop(STRIDE - 1, point)


def barrier_with(axis, offsets):
    me, size = lax.axis_index(axis), lax.axis_size(axis)
    barrier = pltpu.get_barrier_semaphore()
    for d in offsets:
        pl.semaphore_signal(
            barrier, inc=1, device_id={axis: lax.rem(me + d, size)}, device_id_type=MESH
        )
    pl.semaphore_wait(barrier, len(offsets))


def gather_kernel(axis, count, *refs):
    ins, outs = refs[:count], refs[count : 2 * count]
    send, recv, local = refs[2 * count :]
    me, size = lax.axis_index(axis), lax.axis_size(axis)
    barrier_with(axis, range(1, size))
    copies = []
    for d in range(1, size):
        for i in range(count):
            copies.append(
                pltpu.make_async_remote_copy(
                    src_ref=ins[i],
                    dst_ref=outs[i].at[me],
                    send_sem=send.at[i, d - 1],
                    recv_sem=recv.at[i, d - 1],
                    device_id={axis: lax.rem(me + d, size)},
                    device_id_type=MESH,
                )
            )
            copies[-1].start()
    for i in range(count):
        mine = pltpu.make_async_copy(ins[i], outs[i].at[me], local.at[i])
        mine.start()
        copies.append(mine)
    for copy in copies:
        copy.wait()


def gather(axis, arrays, cid):
    size, count = lax.axis_size(axis), len(arrays)
    return pl.pallas_call(
        functools.partial(gather_kernel, axis, count),
        out_shape=[jax.ShapeDtypeStruct((size,) + x.shape, x.dtype) for x in arrays],
        in_specs=[pl.BlockSpec(memory_space=VMEM)] * count,
        out_specs=[pl.BlockSpec(memory_space=VMEM)] * count,
        scratch_shapes=[
            pltpu.SemaphoreType.DMA((count, size - 1)),
            pltpu.SemaphoreType.DMA((count, size - 1)),
            pltpu.SemaphoreType.DMA((count,)),
        ],
        compiler_params=pltpu.CompilerParams(collective_id=cid, has_side_effects=True),
    )(*arrays)


def run_phase(kernel, consts, scalars, arrays, out_shape, scratch):
    smem, vmem = pl.BlockSpec(memory_space=SMEM), pl.BlockSpec(memory_space=VMEM)
    specs = [smem if name in IN_SMEM else vmem for name in CONSTS]
    specs += [smem] * len(scalars) + [vmem] * len(arrays)
    return pl.pallas_call(
        kernel,
        out_shape=out_shape,
        in_specs=specs,
        out_specs=jax.tree.map(lambda _: vmem, out_shape),
        scratch_shapes=scratch,
        compiler_params=pltpu.CompilerParams(vmem_limit_bytes=60 * 1024 * 1024),
    )(*consts, *scalars, *arrays)


def constants(partner, fine_volume, coarse_volume, lift, speed, rates, species):
    elems = partner.shape[0]
    labels = jnp.arange(elems, dtype=jnp.int32)
    hot = (partner[:, :, None] == labels).astype(jnp.bfloat16)
    pick = jnp.transpose(hot.reshape(elems, 3, 2 * elems), (1, 0, 2))
    table = jnp.asarray(face_tables(SIDE)).astype(jnp.bfloat16)
    return (table, pick, lift, fine_volume, coarse_volume, speed, rates, species)


def body(
    coarse_guess,
    initial_state,
    fine_volume,
    coarse_volume,
    lift_matrix,
    wave_speed,
    reaction_rate,
    species_map,
    neighbour_element,
    neighbour_rank,
):
    block, variables, nodes = initial_state.shape
    blocks = lax.axis_size("space")
    elems = block * blocks
    row, col = lax.axis_index("tm"), lax.axis_index("space")
    start = jnp.where(row == 0, initial_state, coarse_guess[0]).astype(jnp.bfloat16)
    partner = jnp.mod(col + neighbour_rank, blocks) * block + neighbour_element
    partner = jnp.pad(partner, ((0, 0), (0, 128 - partner.shape[1])))
    starts, partners = gather("space", [start, partner], 0)
    starts = jnp.transpose(starts.reshape(elems, variables, nodes), (1, 0, 2))
    partners = partners.reshape(elems, 128)[:, :6]
    consts = constants(
        partners, fine_volume, coarse_volume, lift_matrix, wave_speed, reaction_rate, species_map
    )
    scratch = phase_scratch(variables, elems, nodes, lift_matrix.shape[0])
    whole = (variables, elems, nodes)
    half = jax.ShapeDtypeStruct(whole, jnp.bfloat16)
    full = jax.ShapeDtypeStruct(whole, jnp.float32)
    relaxed = run_phase(phase_one, consts, (), (starts,), half, scratch)
    rows = lax.axis_size("tm")
    received = lax.ppermute(relaxed, "tm", [(i, i + 1) for i in range(rows - 1)])
    second = jnp.where(row == 0, starts, received)
    where = jnp.stack([row, col]).astype(jnp.int32)
    corr, message = run_phase(phase_two, consts, (where,), (second,), [full, half], scratch)
    (messages,) = gather("tm", [message], 1)
    out = run_phase(
        phase_three,
        consts,
        (where,),
        (second, corr, messages),
        jax.ShapeDtypeStruct((STRIDE, variables, block, nodes), jnp.float32),
        scratch,
    )
    return jnp.transpose(out, (0, 2, 1, 3))


def solution(mesh):
    placed = (
        P("tm", "space", None, None),
        P("space", None, None),
        P(),
        P(),
        P(),
        P(),
        P(),
        P(),
        P("space", None),
        P("space", None),
    )
    return jax.shard_map(
        body, mesh=mesh, in_specs=placed, out_specs=P("tm", "space", None, None), check_vma=False
    )
```

profile of v0, /device:TPU:15, one launch (start us, length us, event | category | flops | bytes accessed | tf_op | source)
XLA Modules:
  0.0 138.9 jit_solution(6945126717664900484)
XLA Ops:
  0.0 0.1 eq.30
  0.1 0.7 fusion.4
  0.8 0.6 pad.4.refs_1_
  1.4 1.4 copy.25.refs_7_
  2.8 1.9 %fusion.refs_0_ = bf16[8,12,512]{2,1,0:T(8,128)(2,1)} fusion(f32[8,12,512]{2,0,1:T(8,128)} %param.12, f32[1,8,12,512]{3,1,2,0:T(8,128)} %param.11, pred[]{:T(512)S(6)} %eq.26), kind=kLoop, calls=%fused_computation.3 | loop fusion | flops 49152 | bytes 491521 | tf_op jit(solution)/shard_map/convert_element_type | solution.py:265
  4.7 17.1 %shard_map.109 = (bf16[4,8,12,512]{3,2,1,0:T(8,128)(2,1)}, s32[4,8,128]{2,1,0:T(8,128)}) custom-call(bf16[8,12,512]{2,1,0:T(8,128)(2,1)} %fusion.refs_0_, s32[8,128]{1,0:T(8,128)} %pad.4.refs_1_), custom_call_target="tpu_custom_call" | custom-call | tf_op jit(solution)/shard_map/pallas_call | solution.py:212
  21.7 0.0 copy-start
  21.7 0.9 copy.20
  22.6 0.1 copy.21
  22.7 2.0 %copy.31 = bf16[4,8,12,512]{3,1,0,2:T(8,128)(2,1)} copy(bf16[4,8,12,512]{3,2,1,0:T(8,128)(2,1)} %get-tuple-element.10) | data formatting | bytes 786432 | tf_op jit(solution)/shard_map/pallas_call | solution.py:212
  24.7 0.6 fusion.1.refs_1_
  25.3 17.2 %shard_map.110 = bf16[12,32,512]{2,1,0:T(8,128)(2,1)} custom-call(bf16[512,768]{1,0:T(8,128)(2,1)} %constant.33.refs_0_, bf16[3,32,64]{2,1,0:T(8,128)(2,1)} %fusion.1.refs_1_, bf16[384,512]{1,0:T(8,128)(2,1)} %refs_2_.5, bf16[512,512]{1,0:T(8,128)(2,1)} %refs_3_.5, bf16[512,512]{1,0:T(8,128)(2,1)} %refs_4_.5, f32[12]{0:T(128)} %refs_5_.5, f32[24]{0:T(128)} %refs_6_.5, ...), custom_call_target="tpu_custom_call" | custom-call | tf_op jit(solution)/shard_map/pallas_call | solution.py:230
  42.5 1.3 collective-permute-start
  43.8 0.6 pad_add_fusion.refs_8_
  44.4 2.0 %collective-permute-done = bf16[12,32,512]{2,1,0:T(8,128)(2,1)S(1)} collective-permute-done((bf16[12,32,512]{2,1,0:T(8,128)(2,1)}, bf16[12,32,512]{2,1,0:T(8,128)(2,1)S(1)}, u32[]{:S(2)}, u32[]{:S(2)}) %collective-permute-start) | collective-permute-done | bytes 393248 | tf_op jit(solution)/shard_map/ppermute | solution.py:280
  46.3 0.0 copy-done
  46.3 1.0 broadcast_select_fusion.refs_9_
  47.3 19.3 %shard_map.111 = (f32[12,32,512]{2,1,0:T(8,128)}, bf16[12,32,512]{2,1,0:T(8,128)(2,1)}) custom-call(bf16[512,768]{1,0:T(8,128)(2,1)} %constant.33.refs_0_, bf16[3,32,64]{2,1,0:T(8,128)(2,1)} %fusion.1.refs_1_, bf16[384,512]{1,0:T(8,128)(2,1)} %refs_2_.5, bf16[512,512]{1,0:T(8,128)(2,1)} %refs_3_.5, bf16[512,512]{1,0:T(8,128)(2,1)} %refs_4_.5, f32[12]{0:T(128)} %refs_5_.5, ...), custom_call_target="tpu_custom_call" | custom-call | tf_op jit(solution)/shard_map/pallas_call | solution.py:230
  66.7 45.7 %shard_map.112.refs_11_ = bf16[8,12,32,512]{3,2,1,0:T(8,128)(2,1)} custom-call(bf16[12,32,512]{2,1,0:T(8,128)(2,1)} %get-tuple-element.12.refs_0_), custom_call_target="tpu_custom_call" | custom-call | tf_op jit(solution)/shard_map/pallas_call | solution.py:212
  112.3 26.6 %shard_map.113 = f32[4,12,8,512]{3,2,1,0:T(8,128)} custom-call(bf16[512,768]{1,0:T(8,128)(2,1)} %constant.33.refs_0_, bf16[3,32,64]{2,1,0:T(8,128)(2,1)} %fusion.1.refs_1_, bf16[384,512]{1,0:T(8,128)(2,1)} %refs_2_.5, bf16[512,512]{1,0:T(8,128)(2,1)} %refs_3_.5, bf16[512,512]{1,0:T(8,128)(2,1)} %refs_4_.5, f32[12]{0:T(128)} %refs_5_.5, f32[24]{0:T(128)} %refs_6_.5, ...), custom_call_target="tpu_custom_call" | custom-call | tf_op jit(solution)/shard_map/pallas_call | solution.py:230
  (2 shorter events, 0.0 us)
Async XLA Ops:
  21.7 24.6 %copy-start = (bf16[4,8,12,512]{3,2,1,0:T(8,128)(2,1)S(1)}, bf16[4,8,12,512]{3,2,1,0:T(8,128)(2,1)}, u32[]{:S(2)}) copy-start(bf16[4,8,12,512]{3,2,1,0:T(8,128)(2,1)} %get-tuple-element.10) | copy-start | bytes 1179652
  42.5 3.8 %collective-permute-start = (bf16[12,32,512]{2,1,0:T(8,128)(2,1)}, bf16[12,32,512]{2,1,0:T(8,128)(2,1)S(1)}, u32[]{:S(2)}, u32[]{:S(2)}) collective-permute-start(bf16[12,32,512]{2,1,0:T(8,128)(2,1)} %shard_map.110), channel_id=1, source_target_pairs={{0,4},{4,8},{8,12},{12,16},{16,20},{20,24},{24,28},{1,5},{5,9},{9,... | collective-permute-start | bytes 1179656 | tf_op jit(solution)/shard_map/ppermute | solution.py:280
where the time goes:
time: 139 us
  Pallas kernels  126 us (91%)
  local copies, waits for them, and re-layouts  5 us (4%)
  other arithmetic  4.77 us (3%)
  waiting for transfers between devices  1.97 us (1%)
    pallas_call x3, Pallas kernels, run_phase(): pl.pallas_call(kernel, out_shape=out_shape, in_specs=specs, out_specs=jax...  63.1 us
    pallas_call x2, Pallas kernels, gather(): pl.pallas_call(functools.partial(gather_kernel, axis, count), out_shape=[...  62.7 us
  transfers between devices with their start and end apart: 1, of which 1 were waited for; matrix products, arithmetic and copies ran while one was open for 0% of the time, Pallas kernels for 0%

commit v1 on v0

v1 whole, which is shorter than its diff:
```python
import functools

import jax
import jax.numpy as jnp
import numpy as np
from jax import lax
from jax.experimental import pallas as pl
from jax.experimental.pallas import tpu as pltpu
from jax.sharding import PartitionSpec as P

SIDE = 8
STRIDE = 4
COARSE_GAIN = 4.0
VMEM = pltpu.VMEM
SMEM = pltpu.SMEM
MESH = pl.DeviceIdType.MESH


def face_tables(side):
    plane = side * side
    inner = np.arange(plane)
    first, second = inner // side, inner % side
    last = side - 1
    node_lists = [
        first * side + second,
        last * plane + first * side + second,
        first * plane + second,
        first * plane + last * side + second,
        first * plane + second * side,
        first * plane + second * side + last,
    ]
    table = np.zeros((side**3, 12 * plane), np.float32)
    for f in range(6):
        table[node_lists[f], f * plane + inner] = 1.0
        table[node_lists[f ^ 1], (6 + f) * plane + inner] = 1.0
    return table


def find_jumps(speed, c, x_ref, g_ref, j_ref, dims):
    blocks, variables, block, _ = dims
    elems = blocks * block
    faces = c["table"].shape[1] // 2
    plane = faces // 6
    pair = 2 * plane
    both = jnp.dot(x_ref[...], c["table"][...], preferred_element_type=jnp.float32)
    lane = lax.broadcasted_iota(jnp.int32, (1, pair), 1)
    low = jnp.where(lane < plane, 1.0, 0.0)
    high = 1.0 - low

    def first_row(s, v):
        return (s * variables + v) * block

    for k in range(3):
        for v in range(variables):
            swapped = jnp.concatenate(
                [
                    both[
                        first_row(s, v) : first_row(s, v) + block,
                        faces + k * pair : faces + (k + 1) * pair,
                    ]
                    for s in range(blocks)
                ],
                axis=0,
            )
            cols = slice(v * pair, (v + 1) * pair)
            g_ref[k, 0:elems, cols] = (swapped * low).astype(jnp.bfloat16)
            g_ref[k, elems : 2 * elems, cols] = (swapped * high).astype(jnp.bfloat16)
    for k in range(3):
        across = jnp.dot(c["pick"][k], g_ref[k], preferred_element_type=jnp.float32)
        for s in range(blocks):
            for v in range(0, variables, 2):
                parts = []
                for w in (v, v + 1):
                    rows = first_row(s, w)
                    own = both[rows : rows + block, k * pair : (k + 1) * pair]
                    other = across[s * block : (s + 1) * block, w * pair : (w + 1) * pair]
                    parts.append(speed[w] * (other - own))
                rows = first_row(s, v)
                j_ref[rows : rows + 2 * block, k * pair : (k + 1) * pair] = jnp.concatenate(
                    parts, axis=0
                ).astype(jnp.bfloat16)


def transport_react(gain, volume, c, x_ref, j_ref, m_ref, a_ref):
    moved = jnp.dot(x_ref[...], volume[...], preferred_element_type=jnp.float32)
    moved = moved + jnp.dot(j_ref[...], c["lift"][...], preferred_element_type=jnp.float32)
    moved = moved.reshape(m_ref.shape)
    m_ref[...] = moved
    a_ref[...] = moved
    species, rates = c["species"], c["rates"]
    for r in range(species.shape[0]):
        s0, s1, s2 = species[r, 0], species[r, 1], species[r, 2]
        a, b = m_ref[:, s0], m_ref[:, s1]
        rate = (rates[r] * gain) * (a * b) / (1.0 + a * a + b * b)
        a_ref[:, s2] += rate
        a_ref[:, s0] -= rate


def store_state(a_ref, x_ref):
    x_ref[...] = a_ref[...].reshape(x_ref.shape).astype(jnp.bfloat16)


CONSTS = ("table", "partner", "lift", "fine", "coarse", "speed", "rates", "species")
IN_SMEM = ("speed", "rates", "species")


def phase_scratch(dims, faces):
    blocks, variables, block, nodes = dims
    rows, elems = blocks * variables * block, blocks * block
    return [
        VMEM((3, elems, 2 * elems), jnp.bfloat16),
        VMEM((rows, nodes), jnp.bfloat16),
        VMEM((3, 2 * elems, variables * (faces // 3)), jnp.bfloat16),
        VMEM((rows, faces), jnp.bfloat16),
        VMEM(dims, jnp.float32),
        VMEM(dims, jnp.float32),
    ]


def make_pick(partner_ref, pick_ref):
    _, elems, wide = pick_ref.shape
    partner = partner_ref[...].reshape(elems, partner_ref.shape[-1])
    lane = lax.broadcasted_iota(jnp.int32, (elems, wide), 1)
    for k in range(3):
        wanted = jnp.where(
            lane < elems, partner[:, 2 * k : 2 * k + 1], partner[:, 2 * k + 1 : 2 * k + 2] + elems
        )
        pick_ref[k] = jnp.where(lane == wanted, 1.0, 0.0).astype(jnp.bfloat16)


def begin(refs, count):
    c = dict(zip(CONSTS, refs))
    others = refs[len(CONSTS) : len(CONSTS) + count]
    scratch = refs[len(CONSTS) + count :]
    c["pick"] = scratch[0]
    make_pick(c["partner"], c["pick"])
    return c, others, scratch[1:]


def fine_substep(c, x, g, j, m, a):
    find_jumps(c["speed"], c, x, g, j, m.shape)
    transport_react(1.0, c["fine"], c, x, j, m, a)
    store_state(a, x)


def loop(count, fn):
    def one(i, carry):
        fn(i)
        return carry

    lax.fori_loop(0, count, one, 0)


def phase_one(*refs):
    c, (start, out), (x, g, j, m, a) = begin(refs, 2)
    x[...] = start[...].reshape(x.shape)
    loop(2 * STRIDE, lambda i: fine_substep(c, x, g, j, m, a))
    out[...] = x[...].reshape(out.shape)


def phase_two(*refs):
    c, (row, second, corr, message), (x, g, j, m, a) = begin(refs, 4)
    x[...] = second[...].reshape(x.shape)
    find_jumps(c["speed"], c, x, g, j, m.shape)
    transport_react(COARSE_GAIN, c["coarse"], c, x, j, m, a)
    corr[...] = a[...]
    loop(2 * STRIDE, lambda i: fine_substep(c, x, g, j, m, a))
    keep = jnp.where(row[0] == 1, 0.0, 1.0)
    message[...] = (a[...] - keep * corr[...]).reshape(message.shape).astype(jnp.bfloat16)
    corr[...] = a[...] - corr[...]


def phase_three(*refs):
    c, (row, second, corr, messages, out), (x, g, j, m, a) = begin(refs, 5)
    here, own = row[0], row[1]

    @pl.when(here < 2)
    def _():
        x[...] = second[...].reshape(x.shape)

    @pl.when(here >= 2)
    def _():
        x[...] = messages[1].reshape(x.shape)

    def coarse():
        find_jumps(c["speed"], c, x, g, j, m.shape)
        transport_react(COARSE_GAIN, c["coarse"], c, x, j, m, a)

    def advance(i, carry):
        coarse()
        x[...] = (
            a[...].reshape(x.shape) + messages[i].reshape(x.shape).astype(jnp.float32)
        ).astype(jnp.bfloat16)
        return carry

    lax.fori_loop(2, here, advance, 0)
    coarse()
    out[STRIDE - 1] = a[own] + corr[own]

    def point(k):
        loop(2, lambda i: fine_substep(c, x, g, j, m, a))
        out[k] = a[own]

    loop(STRIDE - 1, point)


def greet(axis):
    me, size = lax.axis_index(axis), lax.axis_size(axis)
    barrier = pltpu.get_barrier_semaphore()
    for d in range(1, size):
        pl.semaphore_signal(
            barrier, inc=1, device_id={axis: lax.rem(me + d, size)}, device_id_type=MESH
        )
    pl.semaphore_wait(barrier, size - 1)


def remote(src, dst, send, recv, axis, target):
    return pltpu.make_async_remote_copy(
        src_ref=src,
        dst_ref=dst,
        send_sem=send,
        recv_sem=recv,
        device_id={axis: target},
        device_id_type=MESH,
    )


def start_kernel(guess, initial, partner, starts, partners, mine, send, recv, local):
    me, size = lax.axis_index("space"), lax.axis_size("space")
    block, variables, _ = initial.shape
    first = lax.axis_index("tm") == 0

    def take(ref):
        for v in range(0, variables, 2):
            both = jnp.concatenate([ref[:, v, :], ref[:, v + 1, :]], axis=0)
            mine[v * block : (v + 2) * block, :] = both.astype(jnp.bfloat16)

    @pl.when(first)
    def _():
        take(initial)

    @pl.when(jnp.logical_not(first))
    def _():
        take(guess.at[0])

    greet("space")
    pairs = ((mine, starts), (partner, partners))
    copies = []
    for d in range(1, size):
        for i, (src, dst) in enumerate(pairs):
            copies.append(
                remote(
                    src,
                    dst.at[me],
                    send.at[i, d - 1],
                    recv.at[i, d - 1],
                    "space",
                    lax.rem(me + d, size),
                )
            )
            copies[-1].start()
    for i, (src, dst) in enumerate(pairs):
        copies.append(pltpu.make_async_copy(src, dst.at[me], local.at[i]))
        copies[-1].start()
    for copy in copies:
        copy.wait()


def shift_kernel(relaxed, starts, second, send, recv, local):
    me, size = lax.axis_index("tm"), lax.axis_size("tm")
    blocks = relaxed.shape[0]
    greet("tm")

    def copy(q):
        target = lax.rem(me + 1, size)
        return remote(relaxed.at[q], second.at[q], send.at[q], recv.at[q], "tm", target)

    keep = pltpu.make_async_copy(starts, second, local)

    @pl.when(me < size - 1)
    def _():
        for q in range(blocks):
            copy(q).start()

    @pl.when(me == 0)
    def _():
        keep.start()
        keep.wait()

    @pl.when(me > 0)
    def _():
        for q in range(blocks):
            copy(q).wait_recv()

    @pl.when(me < size - 1)
    def _():
        for q in range(blocks):
            copy(q).wait_send()


def spread_kernel(message, messages, send, pass_send, recv):
    me, size = lax.axis_index("tm"), lax.axis_size("tm")
    chip, core = me // 2, me % 2
    blocks = message.shape[0]
    sibling = me + 1 - 2 * core
    greet("tm")

    def out_copy(slot, q, target):
        return remote(
            message.at[q], messages.at[me, q], send.at[slot, q], recv.at[me, q], "tm", target
        )

    def pass_copy(k, q):
        return remote(
            messages.at[k, q], messages.at[k, q], pass_send.at[k, q], recv.at[k, q], "tm", sibling
        )

    def outgoing(act):
        for p in range(size // 2 - 1, 0, -1):

            @pl.when(jnp.logical_and(me >= 1, chip < p))
            def _():
                for q in range(blocks):
                    act(out_copy(p, q, 2 * p + core))

        @pl.when(jnp.logical_and(me >= 2, core == 0))
        def _():
            for q in range(blocks):
                act(out_copy(0, q, me + 1))

    outgoing(lambda copy: copy.start())
    for k in range(1, size - 1):

        @pl.when(me > k)
        def _():
            for q in range(blocks):
                pass_copy(k, q).wait_recv()

                @pl.when(jnp.logical_and(chip > k // 2, core == k % 2))
                def _():
                    pass_copy(k, q).start()

    for k in range(1, size - 1):

        @pl.when(jnp.logical_and(chip > k // 2, core == k % 2))
        def _():
            for q in range(blocks):
                pass_copy(k, q).wait_send()

    outgoing(lambda copy: copy.wait_send())


def transfer(kernel, cid, arrays, outs, scratch):
    return pl.pallas_call(
        kernel,
        out_shape=outs,
        in_specs=[pl.BlockSpec(memory_space=VMEM)] * len(arrays),
        out_specs=jax.tree.map(lambda _: pl.BlockSpec(memory_space=VMEM), outs),
        scratch_shapes=scratch,
        compiler_params=pltpu.CompilerParams(collective_id=cid, has_side_effects=True),
    )(*arrays)


def run_phase(kernel, consts, scalars, arrays, out_shape, scratch):
    smem, vmem = pl.BlockSpec(memory_space=SMEM), pl.BlockSpec(memory_space=VMEM)
    specs = [smem if name in IN_SMEM else vmem for name in CONSTS]
    specs += [smem] * len(scalars) + [vmem] * len(arrays)
    return pl.pallas_call(
        kernel,
        out_shape=out_shape,
        in_specs=specs,
        out_specs=jax.tree.map(lambda _: vmem, out_shape),
        scratch_shapes=scratch,
        compiler_params=pltpu.CompilerParams(vmem_limit_bytes=60 * 1024 * 1024),
    )(*consts, *scalars, *arrays)


def body(
    coarse_guess,
    initial_state,
    fine_volume,
    coarse_volume,
    lift_matrix,
    wave_speed,
    reaction_rate,
    species_map,
    neighbour_element,
    neighbour_rank,
):
    block, variables, nodes = initial_state.shape
    blocks, rows = lax.axis_size("space"), lax.axis_size("tm")
    row, col = lax.axis_index("tm"), lax.axis_index("space")
    partner = jnp.mod(col + neighbour_rank, blocks) * block + neighbour_element
    partner = jnp.pad(partner, ((0, 0), (0, 128 - partner.shape[1])))
    state = jax.ShapeDtypeStruct((blocks, variables * block, nodes), jnp.bfloat16)
    dma = pltpu.SemaphoreType.DMA
    starts, partners = transfer(
        start_kernel,
        0,
        (coarse_guess, initial_state, partner),
        [state, jax.ShapeDtypeStruct((blocks,) + partner.shape, jnp.int32)],
        [
            VMEM((variables * block, nodes), jnp.bfloat16),
            dma((2, blocks - 1)),
            dma((2, blocks - 1)),
            dma((2,)),
        ],
    )
    table = jnp.asarray(face_tables(SIDE)).astype(jnp.bfloat16)
    consts = (
        table,
        partners,
        lift_matrix,
        fine_volume,
        coarse_volume,
        wave_speed,
        reaction_rate,
        species_map,
    )
    dims = (blocks, variables, block, nodes)
    scratch = phase_scratch(dims, lift_matrix.shape[0])
    relaxed = run_phase(phase_one, consts, (), (starts,), state, scratch)
    second = transfer(
        shift_kernel, 1, (relaxed, starts), state, [dma((blocks,)), dma((blocks,)), dma(())]
    )
    where = jnp.stack([row, col]).astype(jnp.int32)
    corr, message = run_phase(
        phase_two,
        consts,
        (where,),
        (second,),
        [jax.ShapeDtypeStruct(dims, jnp.float32), state],
        scratch,
    )
    messages = transfer(
        spread_kernel,
        2,
        (message,),
        jax.ShapeDtypeStruct((rows,) + state.shape, jnp.bfloat16),
        [dma((rows // 2, blocks)), dma((rows, blocks)), dma((rows, blocks))],
    )
    out = run_phase(
        phase_three,
        consts,
        (where,),
        (second, corr, messages),
        jax.ShapeDtypeStruct((STRIDE, variables, block, nodes), jnp.float32),
        scratch,
    )
    return jnp.transpose(out, (0, 2, 1, 3))


def solution(mesh):
    placed = (
        P("tm", "space", None, None),
        P("space", None, None),
        P(),
        P(),
        P(),
        P(),
        P(),
        P(),
        P("space", None),
        P("space", None),
    )
    return jax.shard_map(
        body, mesh=mesh, in_specs=placed, out_specs=P("tm", "space", None, None), check_vma=False
    )
```

time: 139 us -> 121 us (0.87)
  Pallas kernels: 126 us -> 114 us
  other arithmetic: 4.77 us -> 1.31 us
  waiting for transfers between devices: 1.97 us -> 0 us
    pallas_call x2 -> x3, Pallas kernels: 62.7 us -> 49 us  [transfer(): pl.pallas_call(kernel, out_shape=outs, in_specs=[pl.BlockSpec(memory_spac...]
    unnamed x3, local copies, waits for them, and re-layouts: 1.36 us -> 4.84 us
    pallas_call x1 -> x0, local copies, waits for them, and re-layouts: 2.02 us -> none  [gather(): pl.pallas_call(functools.partial(gather_kernel, axis, count), out_shape=[...]
    ppermute x1 -> x0, waiting for transfers between devices: 1.97 us -> none  [body(): lax.ppermute(relaxed, 'tm', [(i, i + 1) for i in range(rows - 1)])]
    convert_element_type x1 -> x0, other arithmetic: 1.89 us -> none  [body(): jnp.where(row == 0, initial_state, coarse_guess[0]).astype(jnp.bfloat16)]
    pallas_call x3, Pallas kernels: 63.1 us -> 64.5 us  [run_phase(): pl.pallas_call(kernel, out_shape=out_shape, in_specs=specs, out_specs=jax...]
  transfers between devices with their start and end apart: 1 -> 0, of which waited for: 1 -> 0; matrix products, arithmetic and copies ran while one was open for 0% -> 0% of each run, Pallas kernels for 0% -> 0%
where the time goes in v1:
time: 121 us; the launch traced here: 120 us
  Pallas kernels  114 us (94%)
  local copies, waits for them, and re-layouts  5.43 us (4%)
  other arithmetic  1.31 us (1%)
    pallas_call x3, Pallas kernels, run_phase(): pl.pallas_call(kernel, out_shape=out_shape, in_specs=specs, out_specs=jax...  64.5 us
    pallas_call x3, Pallas kernels, transfer(): pl.pallas_call(kernel, out_shape=outs, in_specs=[pl.BlockSpec(memory_spac...  49 us
    unnamed x3, local copies, waits for them, and re-layouts  4.84 us

profile of v1, /device:TPU:15, one launch (start us, length us, event | category | flops | bytes accessed | tf_op | source)
XLA Modules:
  0.0 120.3 jit_solution(5133043137797964230)
XLA Ops:
  0.0 0.6 pad_add_fusion.refs_8_
  0.6 0.7 fusion.2
  1.3 0.6 pad.4.partner
  1.9 1.4 %copy.16.refs_7_ = s32[24,3]{1,0:T(8,128)} copy(s32[24,3]{0,1:T(4,128)} %param.18) | data formatting | bytes 576 | tf_op args[7]
  3.2 1.7 %copy.12.guess = f32[1,8,12,512]{3,2,1,0:T(8,128)} copy(f32[1,8,12,512]{3,1,2,0:T(8,128)} %param.11) | data formatting | bytes 393216 | tf_op args[0]
  5.0 1.7 %copy.13.initial = f32[8,12,512]{2,1,0:T(8,128)} copy(f32[8,12,512]{2,0,1:T(8,128)} %param.12) | data formatting | bytes 393216 | tf_op args[1]
  6.7 14.3 %shard_map.109 = (bf16[4,96,512]{2,1,0:T(8,128)(2,1)}, s32[4,8,128]{2,1,0:T(8,128)}) custom-call(f32[1,8,12,512]{3,2,1,0:T(8,128)} %copy.12.guess, f32[8,12,512]{2,1,0:T(8,128)} %copy.13.initial, s32[8,128]{1,0:T(8,128)} %pad.4.partner), custom_call_target="tpu_custom_call" | custom-call | tf_op jit(solution)/shard_map/pallas_call | solution.py:354
  21.1 17.7 %shard_map.110.relaxed = bf16[4,96,512]{2,1,0:T(8,128)(2,1)} custom-call(bf16[512,768]{1,0:T(8,128)(2,1)} %constant.33.refs_0_, s32[4,8,128]{2,1,0:T(8,128)} %get-tuple-element.9.refs_1_, bf16[384,512]{1,0:T(8,128)(2,1)} %refs_2_.5, bf16[512,512]{1,0:T(8,128)(2,1)} %refs_3_.5, bf16[512,512]{1,0:T(8,128)(2,1)} %refs_4_.5, f32[12]{0:T(128)} %refs_5_.5, ...), custom_call_target="tpu_custom_call" | custom-call | tf_op jit(solution)/shard_map/pallas_call | solution.py:368
  38.8 4.2 %shard_map.111.refs_9_ = bf16[4,96,512]{2,1,0:T(8,128)(2,1)} custom-call(bf16[4,96,512]{2,1,0:T(8,128)(2,1)} %shard_map.110.relaxed, bf16[4,96,512]{2,1,0:T(8,128)(2,1)} %get-tuple-element.10.refs_8_.starts), custom_call_target="tpu_custom_call" | custom-call | tf_op jit(solution)/shard_map/pallas_call | solution.py:354
  43.0 19.8 %shard_map.112 = (f32[4,12,8,512]{3,2,1,0:T(8,128)}, bf16[4,96,512]{2,1,0:T(8,128)(2,1)}) custom-call(bf16[512,768]{1,0:T(8,128)(2,1)} %constant.33.refs_0_, s32[4,8,128]{2,1,0:T(8,128)} %get-tuple-element.9.refs_1_, bf16[384,512]{1,0:T(8,128)(2,1)} %refs_2_.5, bf16[512,512]{1,0:T(8,128)(2,1)} %refs_3_.5, bf16[512,512]{1,0:T(8,128)(2,1)} %refs_4_.5, ...), custom_call_target="tpu_custom_call" | custom-call | tf_op jit(solution)/shard_map/pallas_call | solution.py:368
  62.7 30.4 %shard_map.113.refs_11_ = bf16[8,4,96,512]{3,2,1,0:T(8,128)(2,1)} custom-call(bf16[4,96,512]{2,1,0:T(8,128)(2,1)} %get-tuple-element.12.message), custom_call_target="tpu_custom_call" | custom-call | tf_op jit(solution)/shard_map/pallas_call | solution.py:354
  93.1 27.1 %shard_map.114 = f32[4,12,8,512]{3,2,1,0:T(8,128)} custom-call(bf16[512,768]{1,0:T(8,128)(2,1)} %constant.33.refs_0_, s32[4,8,128]{2,1,0:T(8,128)} %get-tuple-element.9.refs_1_, bf16[384,512]{1,0:T(8,128)(2,1)} %refs_2_.5, bf16[512,512]{1,0:T(8,128)(2,1)} %refs_3_.5, bf16[512,512]{1,0:T(8,128)(2,1)} %refs_4_.5, f32[12]{0:T(128)} %refs_5_.5, f32[24]{0:T(128)} %refs_6_.5, ...), custom_call_target="tpu_custom_call" | custom-call | tf_op jit(solution)/shard_map/pallas_call | solution.py:368

commit v2 on v1

--- a/solution.py
+++ b/solution.py
@@ -82,16 +82,18 @@
 
 
 def transport_react(gain, volume, c, x_ref, j_ref, m_ref, a_ref):
+    h_ref = c["halves"]
     moved = jnp.dot(x_ref[...], volume[...], preferred_element_type=jnp.float32)
     moved = moved + jnp.dot(j_ref[...], c["lift"][...], preferred_element_type=jnp.float32)
     moved = moved.reshape(m_ref.shape)
     m_ref[...] = moved
     a_ref[...] = moved
+    h_ref[...] = moved * moved + 0.5
     species, rates = c["species"], c["rates"]
-    for r in range(species.shape[0]):
-        s0, s1, s2 = species[r, 0], species[r, 1], species[r, 2]
+    for r in range(species.shape[1]):
+        s0, s1, s2 = species[0, r], species[1, r], species[2, r]
         a, b = m_ref[:, s0], m_ref[:, s1]
-        rate = (rates[r] * gain) * (a * b) / (1.0 + a * a + b * b)
+        rate = (rates[r] * gain) * (a * b) / (h_ref[:, s0] + h_ref[:, s1])
         a_ref[:, s2] += rate
         a_ref[:, s0] -= rate
 
@@ -109,6 +111,7 @@
     rows, elems = blocks * variables * block, blocks * block
     return [
         VMEM((3, elems, 2 * elems), jnp.bfloat16),
+        VMEM(dims, jnp.float32),
         VMEM((rows, nodes), jnp.bfloat16),
         VMEM((3, 2 * elems, variables * (faces // 3)), jnp.bfloat16),
         VMEM((rows, faces), jnp.bfloat16),
@@ -119,26 +122,32 @@
 
 def make_pick(partner_ref, pick_ref):
     _, elems, wide = pick_ref.shape
-    partner = partner_ref[...].reshape(elems, partner_ref.shape[-1])
-    lane = lax.broadcasted_iota(jnp.int32, (elems, wide), 1)
-    for k in range(3):
-        wanted = jnp.where(
-            lane < elems, partner[:, 2 * k : 2 * k + 1], partner[:, 2 * k + 1 : 2 * k + 2] + elems
-        )
-        pick_ref[k] = jnp.where(lane == wanted, 1.0, 0.0).astype(jnp.bfloat16)
+    blocks, block, _ = partner_ref.shape
+    lane = lax.broadcasted_iota(jnp.int32, (block, wide), 1)
+    for s in range(blocks):
+        partner = partner_ref[s]
+        for k in range(3):
+            low, high = partner[:, 2 * k : 2 * k + 1], partner[:, 2 * k + 1 : 2 * k + 2]
+            wanted = jnp.where(lane < elems, low, high + elems)
+            hot = jnp.where(lane == wanted, 1.0, 0.0)
+            pick_ref[k, s * block : (s + 1) * block, :] = hot.astype(jnp.bfloat16)
 
 
 def begin(refs, count):
     c = dict(zip(CONSTS, refs))
     others = refs[len(CONSTS) : len(CONSTS) + count]
     scratch = refs[len(CONSTS) + count :]
-    c["pick"] = scratch[0]
+    c["pick"], c["halves"] = scratch[:2]
     make_pick(c["partner"], c["pick"])
-    return c, others, scratch[1:]
+    return c, others, scratch[2:]
 
 
 def fine_substep(c, x, g, j, m, a):
     find_jumps(c["speed"], c, x, g, j, m.shape)
+    fine_rest(c, x, j, m, a)
+
+
+def fine_rest(c, x, j, m, a):
     transport_react(1.0, c["fine"], c, x, j, m, a)
     store_state(a, x)
 
@@ -159,20 +168,21 @@
 
 
 def phase_two(*refs):
-    c, (row, second, corr, message), (x, g, j, m, a) = begin(refs, 4)
+    c, (second, corr, message), (x, g, j, m, a) = begin(refs, 3)
     x[...] = second[...].reshape(x.shape)
     find_jumps(c["speed"], c, x, g, j, m.shape)
     transport_react(COARSE_GAIN, c["coarse"], c, x, j, m, a)
     corr[...] = a[...]
-    loop(2 * STRIDE, lambda i: fine_substep(c, x, g, j, m, a))
-    keep = jnp.where(row[0] == 1, 0.0, 1.0)
+    fine_rest(c, x, j, m, a)
+    loop(2 * STRIDE - 1, lambda i: fine_substep(c, x, g, j, m, a))
+    keep = jnp.where(lax.axis_index("tm") == 1, 0.0, 1.0)
     message[...] = (a[...] - keep * corr[...]).reshape(message.shape).astype(jnp.bfloat16)
     corr[...] = a[...] - corr[...]
 
 
 def phase_three(*refs):
-    c, (row, second, corr, messages, out), (x, g, j, m, a) = begin(refs, 5)
-    here, own = row[0], row[1]
+    c, (second, corr, messages, out), (x, g, j, m, a) = begin(refs, 4)
+    here, own = lax.axis_index("tm"), lax.axis_index("space")
 
     @pl.when(here < 2)
     def _():
@@ -197,11 +207,16 @@
     coarse()
     out[STRIDE - 1] = a[own] + corr[own]
 
-    def point(k):
-        loop(2, lambda i: fine_substep(c, x, g, j, m, a))
-        out[k] = a[own]
-
-    loop(STRIDE - 1, point)
+    fine_rest(c, x, j, m, a)
+
+    def point(i):
+        fine_substep(c, x, g, j, m, a)
+
+        @pl.when(i % 2 == 0)
+        def _():
+            out[i // 2] = a[own]
+
+    loop(2 * (STRIDE - 1) - 1, point)
 
 
 def greet(axis):
@@ -225,14 +240,19 @@
     )
 
 
-def start_kernel(guess, initial, partner, starts, partners, mine, send, recv, local):
+def start_kernel(
+    guess, initial, element, rank, starts, partners, mine, partner, send, recv, local
+):
     me, size = lax.axis_index("space"), lax.axis_size("space")
-    block, variables, _ = initial.shape
+    variables, block, _ = initial.shape
     first = lax.axis_index("tm") == 0
+    partner[...] = jnp.zeros(partner.shape, jnp.int32)
+    other = lax.rem(me + rank[...] + size, size) * block + element[...]
+    partner[:, 0 : other.shape[1]] = other
 
     def take(ref):
         for v in range(0, variables, 2):
-            both = jnp.concatenate([ref[:, v, :], ref[:, v + 1, :]], axis=0)
+            both = jnp.concatenate([ref[v], ref[v + 1]], axis=0)
             mine[v * block : (v + 2) * block, :] = both.astype(jnp.bfloat16)
 
     @pl.when(first)
@@ -389,18 +409,21 @@
 ):
     block, variables, nodes = initial_state.shape
     blocks, rows = lax.axis_size("space"), lax.axis_size("tm")
-    row, col = lax.axis_index("tm"), lax.axis_index("space")
-    partner = jnp.mod(col + neighbour_rank, blocks) * block + neighbour_element
-    partner = jnp.pad(partner, ((0, 0), (0, 128 - partner.shape[1])))
     state = jax.ShapeDtypeStruct((blocks, variables * block, nodes), jnp.bfloat16)
     dma = pltpu.SemaphoreType.DMA
     starts, partners = transfer(
         start_kernel,
         0,
-        (coarse_guess, initial_state, partner),
-        [state, jax.ShapeDtypeStruct((blocks,) + partner.shape, jnp.int32)],
+        (
+            jnp.transpose(coarse_guess, (0, 2, 1, 3)),
+            jnp.transpose(initial_state, (1, 0, 2)),
+            neighbour_element,
+            neighbour_rank,
+        ),
+        [state, jax.ShapeDtypeStruct((blocks, block, 128), jnp.int32)],
         [
             VMEM((variables * block, nodes), jnp.bfloat16),
+            VMEM((block, 128), jnp.int32),
             dma((2, blocks - 1)),
             dma((2, blocks - 1)),
             dma((2,)),
@@ -415,7 +438,7 @@
         coarse_volume,
         wave_speed,
         reaction_rate,
-        species_map,
+        jnp.transpose(species_map),
     )
     dims = (blocks, variables, block, nodes)
     scratch = phase_scratch(dims, lift_matrix.shape[0])
@@ -423,11 +446,10 @@
     second = transfer(
         shift_kernel, 1, (relaxed, starts), state, [dma((blocks,)), dma((blocks,)), dma(())]
     )
-    where = jnp.stack([row, col]).astype(jnp.int32)
     corr, message = run_phase(
         phase_two,
         consts,
-        (where,),
+        (),
         (second,),
         [jax.ShapeDtypeStruct(dims, jnp.float32), state],
         scratch,
@@ -442,7 +464,7 @@
     out = run_phase(
         phase_three,
         consts,
-        (where,),
+        (),
         (second, corr, messages),
         jax.ShapeDtypeStruct((STRIDE, variables, block, nodes), jnp.float32),
         scratch,

time: 121 us -> 111 us (0.917)
  local copies, waits for them, and re-layouts: 5.43 us -> 0 us
  Pallas kernels: 114 us -> 111 us
  other arithmetic: 1.31 us -> 0 us
    unnamed x3 -> x0, local copies, waits for them, and re-layouts: 4.84 us -> none
    pallas_call x3, Pallas kernels: 64.5 us -> 62 us  [run_phase(): pl.pallas_call(kernel, out_shape=out_shape, in_specs=specs, out_specs=jax...]
where the time goes in v2:
time: 111 us
  Pallas kernels  111 us (100%)
    pallas_call x3, Pallas kernels, run_phase(): pl.pallas_call(kernel, out_shape=out_shape, in_specs=specs, out_specs=jax...  62 us
    pallas_call x3, Pallas kernels, transfer(): pl.pallas_call(kernel, out_shape=outs, in_specs=[pl.BlockSpec(memory_spac...  48.9 us

profile of v2, /device:TPU:15, one launch (start us, length us, event | category | flops | bytes accessed | tf_op | source)
XLA Modules:
  0.0 111.0 jit_solution(4235252217603629818)
XLA Ops:
  0.0 14.3 %shard_map.109 = (bf16[4,96,512]{2,1,0:T(8,128)(2,1)}, s32[4,8,128]{2,1,0:T(8,128)}) custom-call(f32[1,12,8,512]{3,2,1,0:T(8,128)} %bitcast.4, f32[12,8,512]{2,1,0:T(8,128)} %bitcast.5, s32[8,6]{1,0:T(8,128)} %element.1, s32[8,6]{1,0:T(8,128)} %rank.1), custom_call_target="tpu_custom_call" | custom-call | tf_op jit(solution)/shard_map/pallas_call | solution.py:374
  14.3 17.4 %shard_map.110.relaxed = bf16[4,96,512]{2,1,0:T(8,128)(2,1)} custom-call(bf16[512,768]{1,0:T(8,128)(2,1)} %constant.4.refs_0_, s32[4,8,128]{2,1,0:T(8,128)} %get-tuple-element.9.refs_1_, bf16[384,512]{1,0:T(8,128)(2,1)} %refs_2_.5, bf16[512,512]{1,0:T(8,128)(2,1)} %refs_3_.5, bf16[512,512]{1,0:T(8,128)(2,1)} %refs_4_.5, f32[12]{0:T(128)} %refs_5_.5, ...), custom_call_target="tpu_custom_call" | custom-call | tf_op jit(solution)/shard_map/pallas_call | solution.py:388
  31.7 4.2 %shard_map.111.refs_8_ = bf16[4,96,512]{2,1,0:T(8,128)(2,1)} custom-call(bf16[4,96,512]{2,1,0:T(8,128)(2,1)} %shard_map.110.relaxed, bf16[4,96,512]{2,1,0:T(8,128)(2,1)} %get-tuple-element.10.refs_8_.starts), custom_call_target="tpu_custom_call" | custom-call | tf_op jit(solution)/shard_map/pallas_call | solution.py:374
  35.9 18.6 %shard_map.112 = (f32[4,12,8,512]{3,2,1,0:T(8,128)}, bf16[4,96,512]{2,1,0:T(8,128)(2,1)}) custom-call(bf16[512,768]{1,0:T(8,128)(2,1)} %constant.4.refs_0_, s32[4,8,128]{2,1,0:T(8,128)} %get-tuple-element.9.refs_1_, bf16[384,512]{1,0:T(8,128)(2,1)} %refs_2_.5, bf16[512,512]{1,0:T(8,128)(2,1)} %refs_3_.5, bf16[512,512]{1,0:T(8,128)(2,1)} %refs_4_.5, ...), custom_call_target="tpu_custom_call" | custom-call | tf_op jit(solution)/shard_map/pallas_call | solution.py:388
  54.5 30.4 %shard_map.113.refs_10_ = bf16[8,4,96,512]{3,2,1,0:T(8,128)(2,1)} custom-call(bf16[4,96,512]{2,1,0:T(8,128)(2,1)} %get-tuple-element.12.message), custom_call_target="tpu_custom_call" | custom-call | tf_op jit(solution)/shard_map/pallas_call | solution.py:374
  85.0 26.0 %shard_map.114 = f32[4,12,8,512]{3,2,1,0:T(8,128)} custom-call(bf16[512,768]{1,0:T(8,128)(2,1)} %constant.4.refs_0_, s32[4,8,128]{2,1,0:T(8,128)} %get-tuple-element.9.refs_1_, bf16[384,512]{1,0:T(8,128)(2,1)} %refs_2_.5, bf16[512,512]{1,0:T(8,128)(2,1)} %refs_3_.5, bf16[512,512]{1,0:T(8,128)(2,1)} %refs_4_.5, f32[12]{0:T(128)} %refs_5_.5, f32[24]{0:T(128)} %refs_6_.5, ...), custom_call_target="tpu_custom_call" | custom-call | tf_op jit(solution)/shard_map/pallas_call | solution.py:388
